TPU v7x, 32 devices: a whole 2x2x4 slice. The times are simulated.
32 devices in a mesh: sec: 2 (over core), blk: 8 (over z, x), ch: 2 (over y).
Axes of the slice: x: 2, y: 2, z: 4, core: 2. Of those that a mesh axis runs over, the one named last changes fastest.
Arguments:
- voltages: bfloat16 [123, 4096, 2048], P(None, 'blk', ('sec', 'ch')), may hold values from -6 to 6
Outputs:
- visibilities: bfloat16 [16, 2, 4096, 4096], P(('sec', 'ch'), None, 'blk')
All inputs are finite; a program needn't handle non-finite values.
Results may differ from a plain program's by a relative error of at most 0.0082.
Values may be sent and summed in bfloat16 or wider, within the bound.
A program may use at most 384 MiB of HBM per device.

v0:
```python
import math
import jax
import jax.numpy as jnp
from jax import lax
from jax.sharding import PartitionSpec as P

FFT = 2048
TAPS = 4
CH_GRP = 4


def make_window(tap_count, frame_len):
    position = jnp.arange(tap_count * frame_len, dtype=jnp.float32)
    offset = (position - tap_count * frame_len / 2 + 0.5) / frame_len
    taper = 0.5 - 0.5 * jnp.cos(2.0 * jnp.pi * (position + 0.5) / (tap_count * frame_len))
    profile = jnp.sinc(offset) * taper
    profile = profile * jnp.sqrt(frame_len / jnp.sum(profile * profile))
    return profile.reshape(tap_count, frame_len)


def dft_table(frame_len, chan_count, bank_size):
    spacing = bank_size // chan_count
    chosen = jnp.arange(chan_count, dtype=jnp.int32) * spacing + spacing // 2
    phases = jnp.arange(frame_len, dtype=jnp.int32)[:, None] * chosen[None, :] % frame_len
    angles = 2.0 * jnp.pi / frame_len * phases.astype(jnp.float32)
    factor = 1.0 / math.sqrt(frame_len)
    weights = jnp.stack([jnp.cos(angles) * factor, -jnp.sin(angles) * factor], axis=-1)
    return weights.reshape(frame_len, chan_count * 2).astype(jnp.bfloat16)


def pair_block(local_panel, remote_panel, steps):
    grams = jnp.einsum(
        "crti,cqtj->crqij", local_panel, remote_panel, preferred_element_type=jnp.float32
    )
    real_sum = grams[:, 0, 0] + grams[:, 1, 1]
    imag_sum = grams[:, 1, 0] - grams[:, 0, 1]
    return jnp.stack([real_sum, imag_sum], axis=1) / steps


def body(voltages):
    groups = lax.axis_size("sec") * lax.axis_size("ch")
    span_len = voltages.shape[2]
    panel_len = voltages.shape[1]
    steps = voltages.shape[0] - TAPS + 1
    chan_total = CH_GRP * groups
    group_pos = lax.axis_index("sec") * lax.axis_size("ch") + lax.axis_index("ch")
    first = group_pos * span_len
    window = lax.dynamic_slice_in_dim(make_window(TAPS, FFT), first, span_len, 1)
    summed = jnp.zeros((steps, panel_len, span_len), jnp.float32)
    for tap_index in range(TAPS):
        summed = summed + window[tap_index] * voltages[tap_index : tap_index + steps].astype(
            jnp.float32
        )
    filtered = summed.astype(jnp.bfloat16)
    weights = lax.dynamic_slice_in_dim(dft_table(FFT, chan_total, FFT // 2), first, span_len, 0)
    terms = jnp.einsum("tsn,nk->kts", filtered, weights, preferred_element_type=jnp.float32)
    spectra = lax.psum_scatter(
        terms.reshape(CH_GRP * lax.axis_size(("sec", "ch")), 2, steps, panel_len),
        ("sec", "ch"),
        scatter_dimension=0,
        tiled=True,
    ).astype(jnp.bfloat16)
    block = pair_block(spectra, lax.all_gather(spectra, "blk", axis=3, tiled=True), steps)
    return block.astype(jnp.bfloat16)


def solution(mesh):
    return jax.shard_map(
        body,
        mesh=mesh,
        in_specs=(P(None, "blk", ("sec", "ch")),),
        out_specs=P(("sec", "ch"), None, "blk", None),
        check_vma=False,
    )
```

profile of v0, /device:TPU:0, one launch (start us, length us, event | category | flops | bytes accessed | tf_op | source)
XLA Modules:
  0.0 491.0 jit_solution(1568423521587529917)
XLA Ops:
  6.5 0.0 reduce-scatter.2.cloned.1.call-start
  6.5 0.8 fusion.49
  7.4 0.1 select_select_fusion
  7.5 0.1 multiply_add_fusion.1
  8.3 0.1 fusion.52
  8.4 0.6 multiply_convert_fusion.1
  9.0 0.1 copy.10
  9.2 0.1 convert_element_type.47
  9.2 82.8 %fusion.1 = f32[32,120,512]{2,0,1:T(8,128)} fusion(bf16[123,512,512]{2,1,0:T(8,128)(2,1)} %param.1, f32[512]{0:T(512)S(1)} %bitcast.42, f32[512]{0:T(512)S(1)} %bitcast.40, f32[512]{0:T(512)S(1)} %bitcast.41, f32[512]{0:T(512)S(1)} %bitcast.39, bf16[2048,32]{0,1:T(8,128)(2,1)S(1)} %convert_element_type.47, s32[]{:T(128)S(6)} %select_n.62), kind=kOutput, calls=%fused_computation.3 | convolution fusion | flops 2390753280 | bytes 259563520 | tf_op jit(solution)/shard_map/tsn,nk->kts/dot_general | solution.py:56
  92.0 10.9 %copy.17 = f32[32,120,512]{2,1,0:T(8,128)} copy(f32[32,120,512]{2,0,1:T(8,128)} %fusion.1) | data formatting | bytes 15728640 | tf_op jit(solution)/shard_map/reshape | solution.py:58
  102.9 0.0 reduce-scatter.2.cloned.1.call-update
  102.9 0.2 all-gather.2.cloned.1.call-start
  103.1 71.6 %reduce-scatter.2.cloned.1.call-done = f32[4,2,120,512]{3,2,1,0:T(8,128)} async-done(((f32[16,2,120,512]{3,2,1,0:T(8,128)}), f32[4,2,120,512]{3,2,1,0:T(8,128)}) %reduce-scatter.2.cloned.1.call-update) | async-done | bytes 1966096 | tf_op jit(solution)/shard_map/reduce_scatter | solution.py:57
  174.7 2.6 convert_element_type.53
  177.4 0.0 all-gather.2.cloned.1.call-update
  177.4 119.1 %all-gather.2.cloned.1.call-done = bf16[4,2,120,4096]{3,2,1,0:T(8,128)(2,1)} async-done(((bf16[4,2,120,512]{3,2,1,0:T(8,128)(2,1)}), bf16[4,2,120,4096]{3,2,1,0:T(8,128)(2,1)}) %all-gather.2.cloned.1.call-update) | async-done | bytes 7864336 | tf_op jit(solution)/shard_map/all_gather | solution.py:63
  296.5 47.8 %convolution_bitcast_fusion = f32[4,2,2,512,4096]{3,4,1,2,0:T(8,128)} fusion(bf16[4,2,120,4096]{3,2,1,0:T(8,128)(2,1)} %all-gather.2.cloned.1.call-done, bf16[4,2,120,512]{3,2,1,0:T(8,128)(2,1)} %convert_element_type.53), kind=kOutput, calls=%fused_computation.4 | convolution fusion | flops 8053063680 | bytes 143065088 | tf_op jit(solution)/shard_map/crti,cqtj->crqij/dot_general | solution.py:32
  344.3 33.2 %fusion.2 = f32[4,1,512,4096]{2,3,0,1:T(8,128)} fusion(f32[4,2,2,512,4096]{3,4,1,2,0:T(8,128)} %convolution_bitcast_fusion), kind=kLoop, calls=%fused_computation.6 | loop fusion | flops 8388608 | bytes 100663296 | tf_op jit(solution)/shard_map/sub | solution.py:36
  377.5 33.1 %fusion.4 = f32[4,1,512,4096]{2,3,0,1:T(8,128)} fusion(f32[4,2,2,512,4096]{3,4,1,2,0:T(8,128)} %convolution_bitcast_fusion), kind=kLoop, calls=%fused_computation.9 | loop fusion | flops 8388608 | bytes 100663296 | tf_op jit(solution)/shard_map/add | solution.py:35
  410.6 32.9 %fusion = bf16[4,2,512,4096]{2,3,0,1:T(8,128)(2,1)} fusion(f32[4,1,512,4096]{2,3,0,1:T(8,128)} %fusion.2, f32[4,1,512,4096]{2,3,0,1:T(8,128)} %fusion.4), kind=kLoop, calls=%fused_computation.2 | loop fusion | flops 50331648 | bytes 100663296 | tf_op jit(solution)/shard_map/convert_element_type | solution.py:64
  443.5 40.6 %copy.14 = bf16[4,2,512,4096]{3,2,1,0:T(8,128)(2,1)} copy(bf16[4,2,512,4096]{2,3,0,1:T(8,128)(2,1)} %fusion) | data formatting | bytes 67108864 | tf_op jit(solution)/shard_map/convert_element_type | solution.py:64
  (5 shorter events, 0.1 us)
Async XLA Ops:
  6.5 168.2 %reduce-scatter.2.cloned.1.call-start = ((), (), s32[]{:S(2)}) async-start(), calls=%async_computation.1 | async-start | bytes 9830400 | tf_op jit(solution)/shard_map/reduce_scatter | solution.py:57
  102.9 193.6 %all-gather.2.cloned.1.call-start = ((), (), s32[]{:S(2)}) async-start(), calls=%async_computation.2 | async-start | bytes 8847360 | tf_op jit(solution)/shard_map/all_gather | solution.py:63
Sparse Core Ops, SparseCore 0:
  103.0 71.6 reduce-scatter.1
  177.5 118.9 all-gather.1
where the time goes:
time: 492 us; the launch traced here: 491 us
  waiting for transfers between devices  191 us (39%)
  matrix products  131 us (27%)
  other arithmetic  104 us (21%)
  local copies, waits for them, and re-layouts  51.7 us (11%)
  between operations  14.2 us (3%)
    all_gather x1, waiting for transfers between devices, body(): lax.all_gather(spectra, 'blk', axis=3, tiled=True)  119 us
    dot_general x1, matrix products, body(): jnp.einsum('tsn,nk->kts', filtered, weights, preferred_element_type=jnp.f...  82.8 us
    reduce_scatter x1, waiting for transfers between devices, body(): lax.psum_scatter(terms.reshape(CH_GRP * lax.axis_size(('sec', 'ch')), 2,...  71.6 us
    dot_general x1, matrix products, pair_block(): jnp.einsum('crti,cqtj->crqij', local_panel, remote_panel, preferred_eleme...  47.8 us
    convert_element_type x1, local copies, waits for them, and re-layouts, body(): return block.astype(jnp.bfloat16)  40.6 us
    sub x1, other arithmetic, pair_block(): imag_sum = grams[:, 1, 0] - grams[:, 0, 1]  33.2 us
    add x1, other arithmetic, pair_block(): real_sum = grams[:, 0, 0] + grams[:, 1, 1]  33.1 us
    convert_element_type x1, other arithmetic, body(): return block.astype(jnp.bfloat16)  32.9 us
  transfers between devices with their start and end apart: 2, of which 2 were waited for; matrix products, arithmetic and copies ran while one was open for 0% of the time, Pallas kernels for 0%

commit v1 on v0

--- a/solution.py
+++ b/solution.py
@@ -7,6 +7,18 @@
 FFT = 2048
 TAPS = 4
 CH_GRP = 4
+
+
+def gather_by_bits(array, axis, dim):
+    ways, here = (lax.axis_size(axis), lax.axis_index(axis))
+    grown, reach = (array, 1)
+    while reach < ways:
+        theirs = lax.ppermute(grown, axis, [(d, d ^ reach) for d in range(ways)])
+        mine_first = jnp.concatenate([grown, theirs], axis=dim)
+        theirs_first = jnp.concatenate([theirs, grown], axis=dim)
+        grown = jnp.where(here & reach == 0, mine_first, theirs_first)
+        reach = 2 * reach
+    return grown
 
 
 def make_window(tap_count, frame_len):
@@ -60,7 +72,7 @@
         scatter_dimension=0,
         tiled=True,
     ).astype(jnp.bfloat16)
-    block = pair_block(spectra, lax.all_gather(spectra, "blk", axis=3, tiled=True), steps)
+    block = pair_block(spectra, gather_by_bits(spectra, "blk", 3), steps)
     return block.astype(jnp.bfloat16)
 
 

time: 492 us -> 620 us (1.26)
  waiting for transfers between devices: 191 us -> 304 us
    ppermute x0 -> x3, waiting for transfers between devices: none -> 233 us  [gather_by_bits(): theirs = lax.ppermute(grown, axis, [(d, d ^ reach) for d in range(ways)])]
    all_gather x1 -> x0, waiting for transfers between devices: 119 us -> none  [body(): lax.all_gather(spectra, 'blk', axis=3, tiled=True)]
    select_n x0 -> x2, other arithmetic: none -> 7.03 us  [gather_by_bits(): grown = jnp.where(here & reach == 0, mine_first, theirs_first)]
  transfers between devices with their start and end apart: 2 -> 4, of which waited for: 2 -> 4; matrix products, arithmetic and copies ran while one was open for 0% -> 0% of each run, Pallas kernels for 0% -> 0%
where the time goes in v1:
time: 620 us; the launch traced here: 619 us
  waiting for transfers between devices  304 us (49%)
  matrix products  133 us (21%)
  other arithmetic  110 us (18%)
  local copies, waits for them, and re-layouts  51.7 us (8%)
  between operations  14.2 us (2%)
    ppermute x3, waiting for transfers between devices, gather_by_bits(): theirs = lax.ppermute(grown, axis, [(d, d ^ reach) for d in range(ways)])  233 us
    dot_general x1, matrix products, body(): jnp.einsum('tsn,nk->kts', filtered, weights, preferred_element_type=jnp.f...  82.8 us
    reduce_scatter x1, waiting for transfers between devices, body(): lax.psum_scatter(terms.reshape(CH_GRP * lax.axis_size(('sec', 'ch')), 2,...  71.8 us
    dot_general x1, matrix products, pair_block(): jnp.einsum('crti,cqtj->crqij', local_panel, remote_panel, preferred_eleme...  50.7 us
    convert_element_type x1, local copies, waits for them, and re-layouts, body(): return block.astype(jnp.bfloat16)  40.6 us
    sub x1, other arithmetic, pair_block(): imag_sum = grams[:, 1, 0] - grams[:, 0, 1]  33.2 us
    add x1, other arithmetic, pair_block(): real_sum = grams[:, 0, 0] + grams[:, 1, 1]  33.1 us
    convert_element_type x1, other arithmetic, body(): return block.astype(jnp.bfloat16)  32.9 us
  transfers between devices with their start and end apart: 4, of which 4 were waited for; matrix products, arithmetic and copies ran while one was open for 0% of the time, Pallas kernels for 0%

profile of v1, /device:TPU:0, one launch (start us, length us, event | category | flops | bytes accessed | tf_op | source)
XLA Modules:
  0.0 618.8 jit_solution(7265574243323415943)
XLA Ops:
  6.5 0.0 reduce-scatter.2.cloned.1.call-start
  6.5 0.8 fusion.56
  7.4 0.1 select_select_fusion
  7.5 0.1 multiply_add_fusion.1
  8.3 0.1 fusion.59
  8.4 0.6 multiply_convert_fusion.1
  9.0 0.1 copy.10
  9.2 0.1 convert_element_type.47
  9.2 82.8 %fusion.1 = f32[32,120,512]{2,0,1:T(8,128)} fusion(bf16[123,512,512]{2,1,0:T(8,128)(2,1)} %param.1, f32[512]{0:T(512)S(1)} %bitcast.46, f32[512]{0:T(512)S(1)} %bitcast.44, f32[512]{0:T(512)S(1)} %bitcast.45, f32[512]{0:T(512)S(1)} %bitcast.43, bf16[2048,32]{0,1:T(8,128)(2,1)S(1)} %convert_element_type.47, s32[]{:T(128)S(6)} %select_n.89), kind=kOutput, calls=%fused_computation.3 | convolution fusion | flops 2390753280 | bytes 259563520 | tf_op jit(solution)/shard_map/tsn,nk->kts/dot_general | solution.py:68
  92.0 10.9 %copy.17 = f32[32,120,512]{2,1,0:T(8,128)} copy(f32[32,120,512]{2,0,1:T(8,128)} %fusion.1) | data formatting | bytes 15728640 | tf_op jit(solution)/shard_map/reshape | solution.py:70
  102.9 0.0 reduce-scatter.2.cloned.1.call-update
  102.9 71.8 %reduce-scatter.2.cloned.1.call-done = f32[4,2,120,512]{3,2,1,0:T(8,128)} async-done(((f32[16,2,120,512]{3,2,1,0:T(8,128)}), f32[4,2,120,512]{3,2,1,0:T(8,128)}) %reduce-scatter.2.cloned.1.call-update) | async-done | bytes 1966096 | tf_op jit(solution)/shard_map/reduce_scatter | solution.py:69
  174.7 1.7 convert_element_type.53
  176.4 1.5 collective-permute-start
  177.9 22.1 %collective-permute-done = bf16[4,2,120,512]{3,2,1,0:T(8,128)(2,1)} collective-permute-done((bf16[4,2,120,512]{3,2,1,0:T(8,128)(2,1)S(1)}, bf16[4,2,120,512]{3,2,1,0:T(8,128)(2,1)}, u32[]{:S(2)}, u32[]{:S(2)}) %collective-permute-start) | collective-permute-done | bytes 983072 | tf_op jit(solution)/shard_map/ppermute | solution.py:16
  200.1 2.2 maximum_select_fusion.2
  202.3 1.5 collective-permute-start.1
  203.8 42.3 %collective-permute-done.1 = bf16[4,2,120,1024]{3,2,1,0:T(8,128)(2,1)} collective-permute-done((bf16[4,2,120,1024]{3,2,1,0:T(8,128)(2,1)S(1)}, bf16[4,2,120,1024]{3,2,1,0:T(8,128)(2,1)}, u32[]{:S(2)}, u32[]{:S(2)}) %collective-permute-start.1) | collective-permute-done | bytes 1966112 | tf_op jit(solution)/shard_map/ppermute | solution.py:16
  246.1 4.9 maximum_select_fusion.1
  251.0 2.4 collective-permute-start.2
  253.4 168.1 %collective-permute-done.2 = bf16[4,2,120,2048]{3,2,1,0:T(8,128)(2,1)} collective-permute-done((bf16[4,2,120,2048]{3,2,1,0:T(8,128)(2,1)}, bf16[4,2,120,2048]{3,2,1,0:T(8,128)(2,1)}, u32[]{:S(2)}, u32[]{:S(2)}) %collective-permute-start.2) | collective-permute-done | bytes 3932192 | tf_op jit(solution)/shard_map/ppermute | solution.py:16
  421.4 50.7 %convolution_bitcast_fusion = f32[4,2,2,512,4096]{3,4,1,2,0:T(8,128)} fusion(bf16[4,2,120,2048]{3,2,1,0:T(8,128)(2,1)} %collective-permute-done.2, bf16[4,2,120,2048]{3,2,1,0:T(8,128)(2,1)} %maximum_select_fusion.1, pred[]{:T(512)S(6)} %eq.38, bf16[4,2,120,512]{3,2,1,0:T(8,128)(2,1)S(1)} %convert_element_type.53), kind=kOutput, calls=%fused_computation.4 | convolution fusion | flops 8088453120 | bytes 143065088 | tf_op jit(solution)/shard_map/crti,cqtj->crqij/dot_general | solution.py:44
  472.1 33.2 %fusion.2 = f32[4,1,512,4096]{2,3,0,1:T(8,128)} fusion(f32[4,2,2,512,4096]{3,4,1,2,0:T(8,128)} %convolution_bitcast_fusion), kind=kLoop, calls=%fused_computation.6 | loop fusion | flops 8388608 | bytes 100663296 | tf_op jit(solution)/shard_map/sub | solution.py:48
  505.3 33.1 %fusion.4 = f32[4,1,512,4096]{2,3,0,1:T(8,128)} fusion(f32[4,2,2,512,4096]{3,4,1,2,0:T(8,128)} %convolution_bitcast_fusion), kind=kLoop, calls=%fused_computation.9 | loop fusion | flops 8388608 | bytes 100663296 | tf_op jit(solution)/shard_map/add | solution.py:47
  538.4 32.9 %fusion = bf16[4,2,512,4096]{2,3,0,1:T(8,128)(2,1)} fusion(f32[4,1,512,4096]{2,3,0,1:T(8,128)} %fusion.2, f32[4,1,512,4096]{2,3,0,1:T(8,128)} %fusion.4), kind=kLoop, calls=%fused_computation.2 | loop fusion | flops 50331648 | bytes 100663296 | tf_op jit(solution)/shard_map/convert_element_type | solution.py:76
  571.3 40.6 %copy.14 = bf16[4,2,512,4096]{3,2,1,0:T(8,128)(2,1)} copy(bf16[4,2,512,4096]{2,3,0,1:T(8,128)(2,1)} %fusion) | data formatting | bytes 67108864 | tf_op jit(solution)/shard_map/convert_element_type | solution.py:76
  (5 shorter events, 0.1 us)
Async XLA Ops:
  6.5 168.2 %reduce-scatter.2.cloned.1.call-start = ((), (), s32[]{:S(2)}) async-start(), calls=%async_computation.1 | async-start | bytes 9830400 | tf_op jit(solution)/shard_map/reduce_scatter | solution.py:69
  176.4 23.7 %collective-permute-start = (bf16[4,2,120,512]{3,2,1,0:T(8,128)(2,1)S(1)}, bf16[4,2,120,512]{3,2,1,0:T(8,128)(2,1)}, u32[]{:S(2)}, u32[]{:S(2)}) collective-permute-start(bf16[4,2,120,512]{3,2,1,0:T(8,128)(2,1)S(1)} %convert_element_type.53), channel_id=1, source_target_pairs={{0,2},{2,0},{4,6},{6,4},{8,10},{10,8},{12,14},{14,12},{1,3},{3,1},... | collective-permute-start | bytes 2949128 | tf_op jit(solution)/shard_map/ppermute | solution.py:16
  202.3 43.9 %collective-permute-start.1 = (bf16[4,2,120,1024]{3,2,1,0:T(8,128)(2,1)S(1)}, bf16[4,2,120,1024]{3,2,1,0:T(8,128)(2,1)}, u32[]{:S(2)}, u32[]{:S(2)}) collective-permute-start(bf16[4,2,120,1024]{3,2,1,0:T(8,128)(2,1)S(1)} %maximum_select_fusion.2), channel_id=1, source_target_pairs={{0,4},{2,6},{4,0},{6,2},{8,12},{10,14},{12,8},{14,10},{1,5},{3,7},... | collective-permute-start | bytes 5898248 | tf_op jit(solution)/shard_map/ppermute | solution.py:16
  251.0 170.4 %collective-permute-start.2 = (bf16[4,2,120,2048]{3,2,1,0:T(8,128)(2,1)}, bf16[4,2,120,2048]{3,2,1,0:T(8,128)(2,1)}, u32[]{:S(2)}, u32[]{:S(2)}) collective-permute-start(bf16[4,2,120,2048]{3,2,1,0:T(8,128)(2,1)} %maximum_select_fusion.1), channel_id=1, source_target_pairs={{0,8},{2,10},{4,12},{6,14},{8,0},{10,2},{12,4},{14,6},{1,9},{3,11}... | collective-permute-start | bytes 11796488 | tf_op jit(solution)/shard_map/ppermute | solution.py:16
Sparse Core Ops, SparseCore 0:
  103.0 71.6 reduce-scatter.1
